TPU v7x, 32 devices: a whole 2x2x4 slice. The times are simulated.
32 devices in a mesh: shot: 2 (over core), gy: 4 (over y, x), gx: 4 (over z).
Axes of the slice: x: 2, y: 2, z: 4, core: 2. Of those that a mesh axis runs over, the one named last changes fastest.
Arguments:
- fwd_prev: float32 [2, 4, 1024, 512], P('shot', None, 'gy', 'gx'), may hold values from -6 to 6
- fwd_cur: float32 [2, 4, 1024, 512], P('shot', None, 'gy', 'gx'), may hold values from -6 to 6
- adj_late: float32 [2, 4, 1024, 512], P('shot', None, 'gy', 'gx'), may hold values from -6 to 6
- adj_now: float32 [2, 4, 1024, 512], P('shot', None, 'gy', 'gx'), may hold values from -6 to 6
- courant: float32 [4, 1024, 512], P(None, 'gy', 'gx'), may hold values from 0.02 to 0.19
- wavelet: float32 [2, 2], P('shot'), may hold values from -16 to 16
- boxes: int32 [2, 4], P('shot'), may hold values from 0 to 1024, as said below
- sources: int32 [2, 3], P('shot'), may hold values from 0 to 1023, as said below
- slab_top: int32 [1], replicated, may hold values from 0 to 508
Outputs:
- gradient: float32 [2, 512, 256], P(None, 'gy', 'gx')
Inputs may be any that keep to these rules, and one draw needn't show every extreme that they name: `boxes`: shot s's box is y0 <= y < y1, x0 <= x < x1 with y0 < y1 <= 1024, x0 < x1 <= 512, every bound a multiple of 16. `sources`: each shot's source cell (z, y, x) lies in the slab and inside that shot's box.
All inputs are finite; a program needn't handle non-finite values.
Results may differ from a plain program's by a relative error of at most 0.0003.
Values sent between devices are 32-bit elements; how exact they have to be, the bound alone decides.
A program may use at most 128 MiB of HBM per device.

v0:
```python
import jax
import jax.numpy as jnp
from jax import lax
from jax.sharding import PartitionSpec as P

COEFFS = (-205.0 / 72.0, 8.0 / 5.0, -1.0 / 5.0, 8.0 / 315.0, -1.0 / 560.0)


def with_halo(cells, sides, width):
    for axis, dim in sides:
        count = lax.axis_size(axis)
        ends = count - 1
        head = lax.slice_in_dim(cells, 0, width, axis=dim)
        tail = lax.slice_in_dim(cells, cells.shape[dim] - width, cells.shape[dim], axis=dim)
        cells = jnp.concatenate(
            [
                lax.ppermute(tail, axis, [(i, (i + 1) % count) for i in range(ends)]),
                cells,
                lax.ppermute(head, axis, [((i + 1) % count, i) for i in range(ends)]),
            ],
            axis=dim,
        )
    return cells


def stencil(padded):
    depth_count = padded.shape[1]
    out_y = padded.shape[2] - 8
    out_x = padded.shape[3] - 8
    deep_pad = jnp.pad(padded[:, :, 4 : 4 + out_y, 4 : 4 + out_x], ((0, 0), (4, 4), (0, 0), (0, 0)))
    summed = 3.0 * COEFFS[0] * deep_pad[:, 4 : 4 + depth_count]
    for offset in range(1, 5):
        neighbours = (
            deep_pad[:, 4 + offset : 4 + offset + depth_count]
            + deep_pad[:, 4 - offset : 4 - offset + depth_count]
        )
        neighbours = neighbours + padded[:, :, 4 + offset : 4 + offset + out_y, 4 : 4 + out_x]
        neighbours = neighbours + padded[:, :, 4 - offset : 4 - offset + out_y, 4 : 4 + out_x]
        neighbours = neighbours + padded[:, :, 4 : 4 + out_y, 4 + offset : 4 + offset + out_x]
        neighbours = neighbours + padded[:, :, 4 : 4 + out_y, 4 - offset : 4 - offset + out_x]
        summed = summed + COEFFS[offset] * neighbours
    return summed


def per_device(fwd_prev, fwd_cur, adj_late, adj_now, courant, wavelet, boxes, sources, slab_top):
    shot_count, depth_count, span_y, span_x = fwd_cur.shape
    anchor_y = lax.axis_index("gy") * span_y
    anchor_x = lax.axis_index("gx") * span_x
    boxes_twice = jnp.concatenate([boxes, boxes], 0)

    def box_mask(margin, box_rows):
        cells_y = anchor_y - margin + jnp.arange(span_y + 2 * margin, dtype=jnp.int32)
        cells_x = anchor_x - margin + jnp.arange(span_x + 2 * margin, dtype=jnp.int32)
        inside_y = (
            (cells_y[None, :] >= box_rows[:, 0:1]) & (cells_y[None, :] < box_rows[:, 1:2])
        ).astype(jnp.float32)
        inside_x = (
            (cells_x[None, :] >= box_rows[:, 2:3]) & (cells_x[None, :] < box_rows[:, 3:4])
        ).astype(jnp.float32)
        return inside_y[:, None, :, None] * inside_x[:, None, None, :]

    def source_term(margin, column):
        cells_y = anchor_y - margin + jnp.arange(span_y + 2 * margin, dtype=jnp.int32)
        cells_x = anchor_x - margin + jnp.arange(span_x + 2 * margin, dtype=jnp.int32)
        cells_z = jnp.arange(depth_count, dtype=jnp.int32)
        onehot_z = (cells_z[None, :] == sources[:, 0:1]).astype(jnp.float32)
        onehot_y = (cells_y[None, :] == sources[:, 1:2]).astype(jnp.float32)
        onehot_x = (cells_x[None, :] == sources[:, 2:3]).astype(jnp.float32)
        weighted = onehot_z * wavelet[:, column : column + 1]
        source_field = (
            weighted[:, :, None, None] * onehot_y[:, None, :, None] * onehot_x[:, None, None, :]
        )
        source_field = jnp.concatenate([source_field, jnp.zeros_like(source_field)], 0)
        return source_field

    stacked_before = jnp.concatenate([fwd_prev, adj_late, courant[None]], 0)
    current = jnp.concatenate([fwd_cur, adj_now], 0)
    older_wide = with_halo(stacked_before, (("gy", 2), ("gx", 3)), 4)
    newer_wide = with_halo(current, (("gy", 2), ("gx", 3)), 8)
    speed_wide = older_wide[2 * shot_count :]
    update = (
        2.0 * newer_wide[:, :, 4:-4, 4:-4]
        - older_wide[: 2 * shot_count]
        + speed_wide * stencil(newer_wide)
    )
    update = update + source_term(4, 0)
    middle = box_mask(4, boxes_twice) * update
    interior = middle[:, :, 4:-4, 4:-4]
    update = 2.0 * interior - current + courant * stencil(middle)
    update = update + source_term(0, 1)
    latest = box_mask(0, boxes_twice) * update
    fwd_mid, adj_mid = (interior[:shot_count], interior[shot_count:])
    fwd_last, adj_first = (latest[:shot_count], latest[shot_count:])
    image_cell = adj_first * (fwd_mid - 2.0 * fwd_cur + fwd_prev) + adj_mid * (
        fwd_last - 2.0 * fwd_mid + fwd_cur
    )
    coarse = image_cell.reshape(
        shot_count, depth_count // 2, 2, span_y // 2, 2, span_x // 2, 2
    ).mean(axis=(2, 4, 6))
    coarse = jnp.sum(coarse, axis=0)
    depth_index = (
        slab_top[0].astype(jnp.float32)
        + 2.0 * jnp.arange(depth_count // 2).astype(jnp.float32)
        + 1.0
    )
    factor = (0.25 + depth_index / 128.0)[:, None, None]
    total = lax.psum(coarse, "shot")
    return total * factor


def solution(mesh):
    return jax.shard_map(
        per_device,
        mesh=mesh,
        in_specs=(
            P("shot", None, "gy", "gx"),
            P("shot", None, "gy", "gx"),
            P("shot", None, "gy", "gx"),
            P("shot", None, "gy", "gx"),
            P(None, "gy", "gx"),
            P("shot", None),
            P("shot", None),
            P("shot", None),
            P(),
        ),
        out_specs=P(None, "gy", "gx"),
        check_vma=False,
    )
```

profile of v0, /device:TPU:0, one launch (start us, length us, event | category | flops | bytes accessed | tf_op | source)
XLA Modules:
  0.0 153.4 jit_solution(927272376209038710)
XLA Ops:
  6.5 1.3 copy.38
  7.8 1.2 copy.39
  9.5 0.3 fusion.62
  9.8 0.3 copy.41
  10.0 5.0 %collective-permute-start.4 = (f32[3,4,4,128]{3,2,1,0:T(4,128)S(1)}, f32[3,4,4,128]{3,2,1,0:T(4,128)S(1)}, u32[]{:S(2)}, u32[]{:S(2)}) collective-permute-start(f32[3,4,4,128]{3,2,1,0:T(4,128)S(1)} %copy.41), channel_id=1, source_target_pairs={{0,4},{4,8},{8,12},{1,5},{5,9},{9,13},{2,6},{6,10},{10,14},{3,7},{... | collective-permute-start | bytes 73736 | tf_op jit(solution)/shard_map/ppermute | solution.py:17
  15.0 0.3 copy.42
  15.3 1.3 collective-permute-start.5
  16.6 1.2 copy.36
  18.1 1.1 fusion.57
  19.2 5.3 %collective-permute-start = (f32[2,4,8,128]{2,3,1,0:T(8,128)}, f32[2,4,8,128]{2,3,1,0:T(8,128)}, u32[]{:S(2)}, u32[]{:S(2)}) collective-permute-start(f32[2,4,8,128]{2,3,1,0:T(8,128)} %get-tuple-element.15), channel_id=1, source_target_pairs={{0,4},{4,8},{8,12},{1,5},{5,9},{9,13},{2,6},{6,10},{10,14},{3,7},{... | collective-permute-start | bytes 98312 | tf_op jit(solution)/shard_map/ppermute | solution.py:17
  24.5 1.3 collective-permute-start.1
  25.9 0.6 fusion.64
  26.5 0.5 compare_convert_fusion.3
  27.0 0.6 compare_convert_fusion.1
  27.6 0.6 compare_convert_fusion.2
  28.3 0.6 compare_convert_fusion
  29.2 0.6 fusion.63
  30.1 0.9 broadcast_multiply_fusion.2
  30.9 1.8 %compare_select_fusion = (f32[4]{0:T(128)S(1)}, f32[4]{0:T(128)S(1)}) fusion(f32[]{:T(128)} %bitcast.6, s32[]{:T(128)} %bitcast.2, f32[]{:T(128)} %bitcast.3), kind=kLoop, calls=%fused_computation.124 | loop fusion | flops 12 | bytes 44 | tf_op jit(solution)/shard_map/mul | solution.py:69
  32.8 1.0 broadcast_multiply_fusion
  33.9 0.9 broadcast_multiply_fusion.1
  34.9 0.8 broadcast_multiply_fusion.3
  36.3 0.3 copy.43
  36.6 1.2 copy.44
  37.8 1.0 pad_maximum_fusion.20
  38.8 3.6 %collective-permute-start.6 = (f32[3,4,264,4]{2,3,1,0:T(4,128)S(1)}, f32[3,4,264,4]{2,3,1,0:T(4,128)S(1)}, u32[]{:S(2)}, u32[]{:S(2)}) collective-permute-start(f32[3,4,264,4]{2,3,1,0:T(4,128)S(1)} %get-tuple-element.9), channel_id=1, source_target_pairs={{0,1},{1,2},{2,3},{4,5},{5,6},{6,7},{8,9},{9,10},{10,11},{12,13},{... | collective-permute-start | bytes 152072 | tf_op jit(solution)/shard_map/ppermute | solution.py:17
  42.5 1.3 collective-permute-start.7
  43.8 5.0 %collective-permute-done.1 = f32[2,4,8,128]{2,3,1,0:T(8,128)} collective-permute-done((f32[2,4,8,128]{2,3,1,0:T(8,128)}, f32[2,4,8,128]{2,3,1,0:T(8,128)}, u32[]{:S(2)}, u32[]{:S(2)}) %collective-permute-start.1) | collective-permute-done | bytes 32800 | tf_op jit(solution)/shard_map/ppermute | solution.py:19
  48.7 0.9 pad_maximum_fusion.12
  49.7 3.5 %collective-permute-start.2 = (f32[2,4,272,8]{2,3,1,0:T(8,128)S(1)}, f32[2,4,272,8]{2,3,1,0:T(8,128)S(1)}, u32[]{:S(2)}, u32[]{:S(2)}) collective-permute-start(f32[2,4,272,8]{2,3,1,0:T(8,128)S(1)} %get-tuple-element.12), channel_id=1, source_target_pairs={{0,1},{1,2},{2,3},{4,5},{5,6},{6,7},{8,9},{9,10},{10,11},{12,13},{... | collective-permute-start | bytes 208904 | tf_op jit(solution)/shard_map/ppermute | solution.py:17
  53.2 1.5 collective-permute-start.3
  54.7 2.5 %pad_maximum_fusion = f32[3,4,264,136]{2,3,1,0:T(8,128)} fusion(f32[3,4,264,4]{2,3,1,0:T(4,128)S(1)} %collective-permute-done.7, f32[3,4,4,128]{2,3,1,0:T(8,128)S(1)} %copy-done, f32[1,4,256,128]{2,3,1,0:T(8,128)S(1)} %bitcast.13, f32[1,4,256,128]{2,3,1,0:T(8,128)S(1)} %copy.40, f32[1,4,256,128]{2,3,1,0:T(8,128)S(1)} %copy.39, ...), kind=kLoop, calls=%fused_computation.12 | loop fusion | flops 2585088 | bytes 3446784 | tf_op jit(solution)/shard_map/concatenate | solution.py:15
  57.2 1.3 maximum_bitcast_fusion
  58.4 1.2 collective-permute-done.3
  59.7 0.6 copy-done.6
  60.3 1.8 %pad_maximum_fusion.1 = f32[2,4,272,144]{2,3,1,0:T(8,128)S(1)} fusion(f32[2,4,272,8]{2,3,1,0:T(8,128)S(1)} %collective-permute-done.3, f32[2,4,8,128]{2,3,1,0:T(8,128)} %collective-permute-done.1, f32[1,4,256,128]{2,3,1,0:T(8,128)S(1)} %copy.37, f32[1,4,256,128]{2,3,1,0:T(8,128)S(1)} %copy.36, f32[2,4,8,128]{2,3,1,0:T(8,128)} %collective-permute-done, ...), kind=kLoop, calls=%fused_computation.13 | loop fusion | flops 1566720 | bytes 2506752 | tf_op jit(solution)/shard_map/concatenate | solution.py:15
  62.2 0.6 slice.299
  62.7 0.4 copy-done.2
  63.2 10.9 %fusion.28 = f32[2,4,264,136]{2,3,1,0:T(8,128)S(1)} fusion(f32[1,4,264,136]{2,3,1,0:T(8,128)} %broadcast_multiply_fusion, f32[2,4,8,128]{2,3,1,0:T(8,128)} %collective-permute-done.1, f32[1,4,256,128]{2,3,1,0:T(8,128)S(1)} %copy.37, f32[1,4,256,128]{2,3,1,0:T(8,128)S(1)} %copy.36, f32[2,4,8,128]{2,3,1,0:T(8,128)} %collective-permute-done, ...), kind=kLoop, calls=%fused_computation.52 | loop fusion | flops 11776512 | bytes 22221312 | tf_op jit(solution)/shard_map/mul | solution.py:87
  74.1 0.4 slice.317
  74.4 0.7 copy-done.1
  75.2 4.3 %fusion.32 = f32[2,4,256,128]{2,3,1,0:T(8,128)S(1)} fusion(f32[1,4,256,128]{2,3,1,0:T(8,128)S(1)} %copy.37, f32[1,4,256,128]{2,3,1,0:T(8,128)S(1)} %copy.36, f32[2,4,256,128]{2,3,1,0:T(8,128)S(1)} %slice.317, f32[2,4,264,136]{2,3,1,0:T(8,128)S(1)} %fusion.28, f32[1,4,256,128]{2,3,1,0:T(8,128)S(1)} %copy-done.1, f32[4,256,128]{1,2,0:T(8,128)S(1)} %copy.38, ...), kind=kLoop, calls=%fused_computation.62 | loop fusion | flops 8912896 | bytes 21233664 | tf_op jit(solution)/shard_map/mul | solution.py:91
  79.5 0.4 fusion.61
  80.1 34.8 %reshape.410 = f32[2,2,128,2,64,2]{5,4,3,2,1,0:T(8,128)} reshape(f32[1,4,256,128]{3,2,1,0:T(8,128)S(1)} %copy.49) | data formatting | bytes 1048576 | tf_op jit(solution)/shard_map/reshape | solution.py:97
  114.9 12.2 %reduce_sum.8 = f32[2,128,64]{2,1,0:T(8,128)S(1)} reduce(f32[2,2,128,2,64,2]{5,4,3,2,1,0:T(8,128)} %reshape.410, f32[]{:T(128)} %constant.23.clone.1), dimensions={1,3,5}, to_apply=%region_0.1 | reduce | flops 114688 | bytes 589828 | tf_op jit(solution)/shard_map/reduce_sum | solution.py:99
  127.3 0.6 broadcast_multiply_fusion.5
  127.9 17.1 %all-reduce.6.cloned.1.call-done = f32[2,128,64]{1,2,0:T(8,128)} async-done(((f32[2,128,64]{1,2,0:T(8,128)}), f32[2,128,64]{1,2,0:T(8,128)}) %all-reduce.6.cloned.1.call-update) | async-done | bytes 65552 | tf_op jit(solution)/shard_map/psum | solution.py:107
  145.0 1.5 %broadcast_multiply_fusion.4 = f32[2,128,64]{1,2,0:T(8,128)} fusion(f32[2,128,64]{1,2,0:T(8,128)} %all-reduce.6.cloned.1.call-done, f32[2]{0:T(128)S(1)} %multiply_add_fusion), kind=kLoop, calls=%fused_computation.111 | loop fusion | flops 16384 | bytes 131080 | tf_op jit(solution)/shard_map/mul | solution.py:108
  (45 shorter events, 1.7 us)
Async XLA Ops:
  6.5 2.6 %copy-start.4 = (f32[1,4,256,128]{3,2,1,0:T(8,128)S(1)}, f32[1,4,256,128]{3,2,1,0:T(8,128)}, u32[]{:S(2)}) copy-start(f32[1,4,256,128]{3,2,1,0:T(8,128)} %param.11) | copy-start | bytes 1572868
  6.5 138.5 %all-reduce.6.cloned.1.call-start = ((), (), s32[]{:S(2)}) async-start(), calls=%async_computation | async-start | bytes 131072 | tf_op jit(solution)/shard_map/psum | solution.py:107
  10.0 7.8 %copy-start.5 = (f32[1,4,256,128]{3,2,1,0:T(8,128)S(1)}, f32[1,4,256,128]{3,2,1,0:T(8,128)}, u32[]{:S(2)}) copy-start(f32[1,4,256,128]{3,2,1,0:T(8,128)} %param.12) | copy-start | bytes 1572868
  10.0 26.3 %collective-permute-start.4 = (f32[3,4,4,128]{3,2,1,0:T(4,128)S(1)}, f32[3,4,4,128]{3,2,1,0:T(4,128)S(1)}, u32[]{:S(2)}, u32[]{:S(2)}) collective-permute-start(f32[3,4,4,128]{3,2,1,0:T(4,128)S(1)} %copy.41), channel_id=1, source_target_pairs={{0,4},{4,8},{8,12},{1,5},{5,9},{9,13},{2,6},{6,10},{10,14},{3,7},{... | collective-permute-start | bytes 73736 | tf_op jit(solution)/shard_map/ppermute | solution.py:17
  15.3 21.3 %collective-permute-start.5 = (f32[3,4,4,128]{3,2,1,0:T(4,128)S(1)}, f32[3,4,4,128]{3,2,1,0:T(4,128)S(1)}, u32[]{:S(2)}, u32[]{:S(2)}) collective-permute-start(f32[3,4,4,128]{3,2,1,0:T(4,128)S(1)} %copy.42), channel_id=1, source_target_pairs={{4,0},{8,4},{12,8},{5,1},{9,5},{13,9},{6,2},{10,6},{14,10},{7,3},{... | collective-permute-start | bytes 73736 | tf_op jit(solution)/shard_map/ppermute | solution.py:19
  17.8 8.0 %copy-start.8 = (s32[1,3]{1,0:T(1,128)S(1)}, s32[1,3]{1,0:T(1,128)}, u32[]{:S(2)}) copy-start(s32[1,3]{1,0:T(1,128)} %param.16) | copy-start | bytes 40
  17.9 11.1 %copy-start.10 = (s32[1,4]{1,0:T(1,128)S(1)}, s32[1,4]{1,0:T(1,128)}, u32[]{:S(2)}) copy-start(s32[1,4]{1,0:T(1,128)} %param.15) | copy-start | bytes 52
  17.9 11.3 %copy-start.9 = (f32[1,2]{1,0:T(1,128)S(1)}, f32[1,2]{1,0:T(1,128)}, u32[]{:S(2)}) copy-start(f32[1,2]{1,0:T(1,128)} %param.14) | copy-start | bytes 28
  19.2 24.6 %collective-permute-start = (f32[2,4,8,128]{2,3,1,0:T(8,128)}, f32[2,4,8,128]{2,3,1,0:T(8,128)}, u32[]{:S(2)}, u32[]{:S(2)}) collective-permute-start(f32[2,4,8,128]{2,3,1,0:T(8,128)} %get-tuple-element.15), channel_id=1, source_target_pairs={{0,4},{4,8},{8,12},{1,5},{5,9},{9,13},{2,6},{6,10},{10,14},{3,7},{... | collective-permute-start | bytes 98312 | tf_op jit(solution)/shard_map/ppermute | solution.py:17
  24.5 24.2 %collective-permute-start.1 = (f32[2,4,8,128]{2,3,1,0:T(8,128)}, f32[2,4,8,128]{2,3,1,0:T(8,128)}, u32[]{:S(2)}, u32[]{:S(2)}) collective-permute-start(f32[2,4,8,128]{2,3,1,0:T(8,128)} %get-tuple-element.16), channel_id=1, source_target_pairs={{4,0},{8,4},{12,8},{5,1},{9,5},{13,9},{6,2},{10,6},{14,10},{7,3},{... | collective-permute-start | bytes 98312 | tf_op jit(solution)/shard_map/ppermute | solution.py:19
  38.8 15.9 %copy-start = (f32[3,4,4,128]{2,3,1,0:T(8,128)S(1)}, f32[3,4,4,128]{2,3,1,0:T(8,128)}, u32[]{:S(2)}) copy-start(f32[3,4,4,128]{2,3,1,0:T(8,128)} %copy.44) | copy-start | bytes 73732
  38.8 15.8 %collective-permute-start.6 = (f32[3,4,264,4]{2,3,1,0:T(4,128)S(1)}, f32[3,4,264,4]{2,3,1,0:T(4,128)S(1)}, u32[]{:S(2)}, u32[]{:S(2)}) collective-permute-start(f32[3,4,264,4]{2,3,1,0:T(4,128)S(1)} %get-tuple-element.9), channel_id=1, source_target_pairs={{0,1},{1,2},{2,3},{4,5},{5,6},{6,7},{8,9},{9,10},{10,11},{12,13},{... | collective-permute-start | bytes 152072 | tf_op jit(solution)/shard_map/ppermute | solution.py:17
  42.5 12.2 %collective-permute-start.7 = (f32[3,4,264,4]{2,3,1,0:T(4,128)S(1)}, f32[3,4,264,4]{2,3,1,0:T(4,128)S(1)}, u32[]{:S(2)}, u32[]{:S(2)}) collective-permute-start(f32[3,4,264,4]{2,3,1,0:T(4,128)S(1)} %get-tuple-element.10), channel_id=1, source_target_pairs={{1,0},{2,1},{3,2},{5,4},{6,5},{7,6},{9,8},{10,9},{11,10},{13,12},{... | collective-permute-start | bytes 152072 | tf_op jit(solution)/shard_map/ppermute | solution.py:19
  49.7 8.8 %collective-permute-start.2 = (f32[2,4,272,8]{2,3,1,0:T(8,128)S(1)}, f32[2,4,272,8]{2,3,1,0:T(8,128)S(1)}, u32[]{:S(2)}, u32[]{:S(2)}) collective-permute-start(f32[2,4,272,8]{2,3,1,0:T(8,128)S(1)} %get-tuple-element.12), channel_id=1, source_target_pairs={{0,1},{1,2},{2,3},{4,5},{5,6},{6,7},{8,9},{9,10},{10,11},{12,13},{... | collective-permute-start | bytes 208904 | tf_op jit(solution)/shard_map/ppermute | solution.py:17
  53.2 6.5 %collective-permute-start.3 = (f32[2,4,272,8]{2,3,1,0:T(8,128)S(1)}, f32[2,4,272,8]{2,3,1,0:T(8,128)S(1)}, u32[]{:S(2)}, u32[]{:S(2)}) collective-permute-start(f32[2,4,272,8]{2,3,1,0:T(8,128)S(1)} %get-tuple-element.11), channel_id=1, source_target_pairs={{1,0},{2,1},{3,2},{5,4},{6,5},{7,6},{9,8},{10,9},{11,10},{13,12},{... | collective-permute-start | bytes 208904 | tf_op jit(solution)/shard_map/ppermute | solution.py:19
  59.7 0.6 copy-start.6
  62.1 1.0 copy-start.2
  62.2 1.0 copy-start.7
  74.1 1.0 copy-start.1
  74.1 1.1 copy-start.3
Sparse Core Ops, SparseCore 0:
  128.1 16.9 all-reduce.5
where the time goes:
time: 154 us; the launch traced here: 153 us
  other arithmetic  47.1 us (31%)
  local copies, waits for them, and re-layouts  45.7 us (30%)
  waiting for transfers between devices  23.3 us (15%)
  starting transfers between devices  22.8 us (15%)
  between operations  14.5 us (9%)
    reshape x1, local copies, waits for them, and re-layouts, per_device(): image_cell.reshape(shot_count, depth_count // 2, 2, span_y // 2, 2, span_...  34.8 us
    ppermute x4, starting transfers between devices, with_halo(): lax.ppermute(tail, axis, [(i, (i + 1) % count) for i in range(ends)])  17.4 us
    psum x1, waiting for transfers between devices, per_device(): total = lax.psum(coarse, 'shot')  17.1 us
    reduce_sum x1, other arithmetic, per_device(): coarse = image_cell.reshape(shot_count, depth_count // 2, 2, span_y // 2,...  12.2 us
    mul x1, other arithmetic, per_device(): middle = box_mask(4, boxes_twice) * update  10.9 us
    ppermute x4, waiting for transfers between devices, with_halo(): lax.ppermute(head, axis, [((i + 1) % count, i) for i in range(ends)])  6.23 us
    unnamed x27, local copies, waits for them, and re-layouts  5.99 us
    ppermute x4, starting transfers between devices, with_halo(): lax.ppermute(head, axis, [((i + 1) % count, i) for i in range(ends)])  5.34 us
  transfers between devices with their start and end apart: 9, of which 3 were waited for; matrix products, arithmetic and copies ran while one was open for 13% of the time, Pallas kernels for 0%

commit v1 on v0

v1 whole, which is shorter than its diff:
```python
import functools

import jax
import jax.numpy as jnp
from jax import lax
from jax.experimental import pallas as pl
from jax.experimental.pallas import tpu as pltpu
from jax.sharding import PartitionSpec as P

COEFFS = (-205.0 / 72.0, 8.0 / 5.0, -1.0 / 5.0, 8.0 / 315.0, -1.0 / 560.0)
MESH = pl.DeviceIdType.MESH
PAD = 8
LANES = 128


def kernel(
    shots, counts, wave_ref, box_ref, src_ref, top_ref, f0_hbm, f1_hbm, a3_hbm, a2_hbm, c_hbm, out_ref,
    now, mid, old, speed, image, strips_out, strips_in, merged, coarse, arrived,
    load_sem, send_sem, recv_sem, shot_send, shot_recv,
):
    county, countx = counts
    nz, ny = speed.shape[0], speed.shape[1]
    half, quarter = ny // 2, ny // 4
    planes = [(f, z) for f in range(2) for z in range(nz)]
    gy, gx, shot = lax.axis_index("gy"), lax.axis_index("gx"), lax.axis_index("shot")
    has_up, has_down = gy > 0, gy < county - 1
    has_left, has_right = gx > 0, gx < countx - 1

    loads = [
        pltpu.make_async_copy(f1_hbm.at[0], now.at[0, :, pl.ds(PAD, ny), :], load_sem.at[0]),
        pltpu.make_async_copy(a2_hbm.at[0], now.at[1, :, pl.ds(PAD, ny), :], load_sem.at[1]),
        pltpu.make_async_copy(c_hbm, speed, load_sem.at[2]),
        pltpu.make_async_copy(f0_hbm.at[0], old.at[0], load_sem.at[3]),
        pltpu.make_async_copy(a3_hbm.at[0], old.at[1], load_sem.at[4]),
    ]
    for load in loads:
        load.start()

    barrier = pltpu.get_barrier_semaphore()
    sides = [
        (has_up, {"gy": gy - 1}),
        (has_down, {"gy": gy + 1}),
        (has_left, {"gx": gx - 1}),
        (has_right, {"gx": gx + 1}),
    ]
    for there, device in sides:
        @pl.when(there)
        def _(device=device):
            pl.semaphore_signal(barrier, inc=1, device_id=device, device_id_type=MESH)
    for step in range(1, shots):
        pl.semaphore_signal(
            barrier, inc=1, device_id={"shot": lax.rem(shot + step, shots)}, device_id_type=MESH
        )
    expected = shots - 1
    for there, _ in sides:
        expected = expected + there.astype(jnp.int32)

    nothing = jnp.zeros((2, nz, PAD, LANES), jnp.float32)
    for there, start in ((has_up, 0), (has_down, PAD + ny)):
        @pl.when(jnp.logical_not(there))
        def _(start=start):
            now[:, :, pl.ds(start, PAD), :] = nothing
            mid[:, :, pl.ds(start, PAD), :] = nothing
    for there, side in ((has_left, 0), (has_right, 1)):
        @pl.when(jnp.logical_not(there))
        def _(side=side):
            strips_in[:, side] = jnp.zeros((2, quarter, LANES), jnp.float32)

    lane = lax.broadcasted_iota(jnp.int32, (8, LANES), 1)
    row = lax.broadcasted_iota(jnp.int32, (8, LANES), 0)
    group = lane // 8
    low = lax.rem(lane, 8) < 4

    def exchange(cells, phase):
        def remote(index, src, dst, device):
            return pltpu.make_async_remote_copy(
                src_ref=src, dst_ref=dst,
                send_sem=send_sem.at[phase, index], recv_sem=recv_sem.at[phase, index],
                device_id=device, device_id_type=MESH,
            )

        first, last = pl.ds(PAD, PAD), pl.ds(ny, PAD)
        above, below = pl.ds(0, PAD), pl.ds(PAD + ny, PAD)
        copies = [
            remote(0, cells.at[:, :, last, :], cells.at[:, :, above, :], {"gy": gy + 1}),
            remote(1, cells.at[:, :, first, :], cells.at[:, :, below, :], {"gy": gy - 1}),
            remote(2, strips_out.at[phase, 0], strips_in.at[phase, 0], {"gx": gx + 1}),
            remote(3, strips_out.at[phase, 1], strips_in.at[phase, 1], {"gx": gx - 1}),
        ]
        to = (has_down, has_up, has_right, has_left)
        came = (has_up, has_down, has_left, has_right)

        def start(which):
            for i in which:
                @pl.when(to[i])
                def _(i=i):
                    copies[i].start()

        def pack(i, carry):
            both = []
            for part in range(2):
                packed = jnp.zeros((8, LANES), jnp.float32)
                for q in range(2):
                    at = pl.multiple_of(i * 8, 8) + PAD + q * half + part * quarter
                    for p, (f, z) in enumerate(planes):
                        base = q * 64 + p * 8
                        moved = pltpu.roll(cells[f, z, pl.ds(at, 8), :], (base + 4) % LANES, 1)
                        packed = jnp.where(group == base // 8, moved, packed)
                both.append(packed)
            rows = pl.ds(pl.multiple_of(i * 8, 8), 8)
            strips_out[phase, 0, rows, :] = jnp.where(low, both[0], pltpu.roll(both[1], 4, 1))
            strips_out[phase, 1, rows, :] = jnp.where(
                low, pltpu.roll(both[0], LANES - 4, 1), both[1]
            )
            return carry

        def merge(i, carry):
            rows = pl.ds(pl.multiple_of(i * 8, 8), 8)
            left, right = strips_in[phase, 0, rows, :], strips_in[phase, 1, rows, :]
            merged[rows, :] = jnp.where(low, left, pltpu.roll(right, 4, 1))
            later = pl.ds(pl.multiple_of(i * 8 + quarter, 8), 8)
            merged[later, :] = jnp.where(low, pltpu.roll(left, LANES - 4, 1), right)
            return carry

        def finish():
            for i in range(4):
                @pl.when(to[i])
                def _(i=i):
                    copies[i].wait_send()
                @pl.when(came[i])
                def _(i=i):
                    copies[i].wait_recv()
            lax.fori_loop(0, quarter // 8, merge, 0)

        return start, pack, finish

    def laplacian(cells, f, at, q, halo):
        centre = [cells[f, z, pl.ds(at + PAD, 8), :] for z in range(nz)]
        result = []
        for z in range(nz):
            u = centre[z]
            base = q * 64 + (f * nz + z) * 8
            h = pltpu.roll(halo, (124 - base) % LANES, 1)
            total = (3.0 * COEFFS[0]) * u
            for k in range(1, 5):
                s = cells[f, z, pl.ds(at + (PAD + k), 8), :] + cells[f, z, pl.ds(at + (PAD - k), 8), :]
                s = s + pltpu.roll(jnp.where(lane < k, h, u), LANES - k, 1)
                s = s + pltpu.roll(jnp.where(lane >= LANES - k, h, u), k, 1)
                if z + k < nz:
                    s = s + centre[z + k]
                if z - k >= 0:
                    s = s + centre[z - k]
                total = total + COEFFS[k] * s
            result.append(total)
        return centre, result

    y0, y1, x0, x1 = box_ref[0, 0], box_ref[0, 1], box_ref[0, 2], box_ref[0, 3]
    sz, sy, sx = src_ref[0, 0], src_ref[0, 1], src_ref[0, 2]
    cell_x = gx * LANES + lane
    inside_x = (cell_x >= x0) & (cell_x < x1)
    source_x = cell_x == sx

    def place(at):
        cell_y = gy * ny + at + row
        inside = inside_x & (cell_y >= y0) & (cell_y < y1)
        return inside, source_x & (cell_y == sy)

    def amplitude(step, z):
        return jnp.where(sz == z, wave_ref[0, step], 0.0)

    def first_step(i, carry):
        halo = merged[pl.ds(pl.multiple_of(i * 8, 8), 8), :]
        for q in range(2):
            at = pl.multiple_of(i * 8 + q * half, 8)
            inside, source = place(at)
            for f in range(2):
                centre, lap = laplacian(now, f, at, q, halo)
                for z in range(nz):
                    new = 2.0 * centre[z] - old[f, z, pl.ds(at, 8), :]
                    new = new + speed[z, pl.ds(at, 8), :] * lap[z]
                    if f == 0:
                        new = new + jnp.where(source, amplitude(0, z), 0.0)
                    mid[f, z, pl.ds(at + PAD, 8), :] = jnp.where(inside, new, 0.0)
        return carry

    def second_step(i, carry):
        halo = merged[pl.ds(pl.multiple_of(i * 8, 8), 8), :]
        for q in range(2):
            at = pl.multiple_of(i * 8 + q * half, 8)
            inside, source = place(at)
            f2, lap_f = laplacian(mid, 0, at, q, halo)
            a1, lap_a = laplacian(mid, 1, at, q, halo)
            total = None
            for z in range(nz):
                c = speed[z, pl.ds(at, 8), :]
                f0 = old[0, z, pl.ds(at, 8), :]
                f1 = now[0, z, pl.ds(at + PAD, 8), :]
                a2 = now[1, z, pl.ds(at + PAD, 8), :]
                bent = f2[z] - 2.0 * f1
                f3 = 2.0 * f2[z] - f1 + c * lap_f[z] + jnp.where(source, amplitude(1, z), 0.0)
                f3 = jnp.where(inside, f3, 0.0)
                a0 = jnp.where(inside, 2.0 * a1[z] - a2 + c * lap_a[z], 0.0)
                part = a0 * (bent + f0) + a1[z] * (f3 - 2.0 * f2[z] + f1)
                total = part if z % 2 == 0 else total + part
                if z % 2 == 1:
                    image[z // 2, pl.ds(at, 8), :] = total
        return carry

    loads[0].wait()
    loads[1].wait()
    pl.semaphore_wait(barrier, expected)
    start, pack, finish = exchange(now, 0)
    start((0, 1))
    lax.fori_loop(0, quarter // 8, pack, 0)
    start((2, 3))
    for load in loads[2:]:
        load.wait()
    finish()
    lax.fori_loop(0, half // 8, first_step, 0)

    start, pack, finish = exchange(mid, 1)
    start((0, 1))
    lax.fori_loop(0, quarter // 8, pack, 0)
    start((2, 3))
    finish()
    lax.fori_loop(0, half // 8, second_step, 0)

    pair = lax.broadcasted_iota(jnp.int32, (LANES, LANES), 0) // 2
    column = lax.broadcasted_iota(jnp.int32, (LANES, LANES), 1)
    total = None
    for k in range(nz // 2):
        rows = image[k, pl.ds(0, half, stride=2), :] + image[k, pl.ds(1, half, stride=2), :]
        pick = (column == pair + 64 * k).astype(jnp.float32)
        part = jnp.dot(rows, pick, precision=lax.Precision.HIGHEST, preferred_element_type=jnp.float32)
        total = part if total is None else total + part
    coarse[...] = total
    sends = []
    for step in range(1, shots):
        copy = pltpu.make_async_remote_copy(
            src_ref=coarse, dst_ref=arrived.at[step - 1],
            send_sem=shot_send.at[step - 1], recv_sem=shot_recv.at[step - 1],
            device_id={"shot": lax.rem(shot + step, shots)}, device_id_type=MESH,
        )
        copy.start()
        sends.append(copy)
    for step, copy in enumerate(sends):
        copy.wait_recv()
        total = total + arrived[step]
    depth = top_ref[0].astype(jnp.float32)
    for k in range(nz // 2):
        factor = (0.25 + (depth + (2.0 * k + 1.0)) / 128.0) * 0.125
        out_ref[k] = total[:, 64 * k : 64 * k + 64] * factor
    for copy in sends:
        copy.wait_send()


def per_device(shots, counts, fwd_prev, fwd_cur, adj_late, adj_now, courant, wavelet, boxes, sources, slab_top):
    nz, ny, nx = courant.shape
    f32 = jnp.float32
    smem = pl.BlockSpec(memory_space=pltpu.SMEM)
    hbm = pl.BlockSpec(memory_space=pl.ANY)
    return pl.pallas_call(
        functools.partial(kernel, shots, counts),
        out_shape=jax.ShapeDtypeStruct((nz // 2, ny // 2, nx // 2), f32),
        in_specs=[smem] * 4 + [hbm] * 5,
        out_specs=pl.BlockSpec(memory_space=pltpu.VMEM),
        scratch_shapes=[
            pltpu.VMEM((2, nz, ny + 2 * PAD, nx), f32),
            pltpu.VMEM((2, nz, ny + 2 * PAD, nx), f32),
            pltpu.VMEM((2, nz, ny, nx), f32),
            pltpu.VMEM((nz, ny, nx), f32),
            pltpu.VMEM((nz // 2, ny, nx), f32),
            pltpu.VMEM((2, 2, ny // 4, nx), f32),
            pltpu.VMEM((2, 2, ny // 4, nx), f32),
            pltpu.VMEM((ny // 2, nx), f32),
            pltpu.VMEM((ny // 2, nx), f32),
            pltpu.VMEM((max(shots - 1, 1), ny // 2, nx), f32),
            pltpu.SemaphoreType.DMA((5,)),
            pltpu.SemaphoreType.DMA((2, 4)),
            pltpu.SemaphoreType.DMA((2, 4)),
            pltpu.SemaphoreType.DMA((max(shots - 1, 1),)),
            pltpu.SemaphoreType.DMA((max(shots - 1, 1),)),
        ],
        compiler_params=pltpu.CompilerParams(
            collective_id=0, has_side_effects=True, vmem_limit_bytes=32 * 1024 * 1024
        ),
    )(wavelet, boxes, sources, slab_top, fwd_prev, fwd_cur, adj_late, adj_now, courant)


def solution(mesh):
    shots = mesh.shape["shot"]
    counts = (mesh.shape["gy"], mesh.shape["gx"])
    return jax.shard_map(
        functools.partial(per_device, shots, counts),
        mesh=mesh,
        in_specs=(
            P("shot", None, "gy", "gx"),
            P("shot", None, "gy", "gx"),
            P("shot", None, "gy", "gx"),
            P("shot", None, "gy", "gx"),
            P(None, "gy", "gx"),
            P("shot", None),
            P("shot", None),
            P("shot", None),
            P(),
        ),
        out_specs=P(None, "gy", "gx"),
        check_vma=False,
    )
```

time: 154 us -> 33.4 us (0.22)
  other arithmetic: 47.1 us -> 0 us
  local copies, waits for them, and re-layouts: 45.7 us -> 5.92 us
  Pallas kernels: 0 us -> 26.4 us
  waiting for transfers between devices: 23.3 us -> 0 us
  starting transfers between devices: 22.8 us -> 0 us
  between operations: 14.5 us -> 0.74 us
    reshape x1 -> x0, local copies, waits for them, and re-layouts: 34.8 us -> none  [per_device(): image_cell.reshape(shot_count, depth_count // 2, 2, span_y // 2, 2, span_...]
    pallas_call x0 -> x1, Pallas kernels: none -> 26.4 us  [per_device(): pl.pallas_call(functools.partial(kernel, shots, counts), out_shape=jax.Sh...]
    mul x11 -> x0, other arithmetic: 23.6 us -> none  [the longest x1 10.9 us: per_device(): middle = box_mask(4, boxes_twice) * update]
    ppermute x8 -> x0, starting transfers between devices: 22.8 us -> none  [the longest x4 17.4 us: with_halo(): lax.ppermute(tail, axis, [(i, (i + 1) % count) for i in range(ends)])]
    psum x1 -> x0, waiting for transfers between devices: 17.1 us -> none  [per_device(): total = lax.psum(coarse, 'shot')]
    reduce_sum x1 -> x0, other arithmetic: 12.2 us -> none  [per_device(): coarse = image_cell.reshape(shot_count, depth_count // 2, 2, span_y // 2,...]
    concatenate x6 -> x0, other arithmetic: 6.5 us -> none  [the longest x3 5.2 us: with_halo(): jnp.concatenate([lax.ppermute(tail, axis, [(i, (i + 1) % count) for i in...]
    ppermute x8 -> x0, waiting for transfers between devices: 6.24 us -> none  [the longest x4 6.23 us: with_halo(): lax.ppermute(head, axis, [((i + 1) % count, i) for i in range(ends)])]
  transfers between devices with their start and end apart: 9 -> 0, of which waited for: 3 -> 0; matrix products, arithmetic and copies ran while one was open for 13% -> 0% of each run, Pallas kernels for 0% -> 0%
where the time goes in v1:
time: 33.4 us; the launch traced here: 33.1 us
  Pallas kernels  26.4 us (79%)
  local copies, waits for them, and re-layouts  5.92 us (18%)
  between operations  0.74 us (2%)
    pallas_call x1, Pallas kernels, per_device(): pl.pallas_call(functools.partial(kernel, shots, counts), out_shape=jax.Sh...  26.4 us
    unnamed x16, local copies, waits for them, and re-layouts  5.21 us
    pallas_call x1, local copies, waits for them, and re-layouts, per_device(): pl.pallas_call(functools.partial(kernel, shots, counts), out_shape=jax.Sh...  0.71 us

profile of v1, /device:TPU:0, one launch (start us, length us, event | category | flops | bytes accessed | tf_op | source)
XLA Modules:
  0.0 33.1 jit_solution(12627933686116113017)
XLA Ops:
  0.0 0.0 copy-start.7
  0.0 0.0 copy-start.6
  0.0 0.0 copy-start.5
  0.7 0.0 copy-done.7
  0.7 0.0 copy-done.6
  0.7 0.0 copy-done.5
  0.7 0.0 copy-start
  0.7 1.0 %copy-done = f32[1,4,256,128]{3,2,1,0:T(8,128)S(1)} copy-done((f32[1,4,256,128]{3,2,1,0:T(8,128)S(1)}, f32[1,4,256,128]{3,2,1,0:T(8,128)}, u32[]{:S(2)}) %copy-start) | copy-done | bytes 524312
  1.8 0.0 copy-start.1
  1.8 1.0 %copy-done.1 = f32[1,4,256,128]{3,2,1,0:T(8,128)S(1)} copy-done((f32[1,4,256,128]{3,2,1,0:T(8,128)S(1)}, f32[1,4,256,128]{3,2,1,0:T(8,128)}, u32[]{:S(2)}) %copy-start.1) | copy-done | bytes 524312
  2.8 0.0 copy-start.2
  2.8 1.0 %copy-done.2 = f32[1,4,256,128]{3,2,1,0:T(8,128)S(1)} copy-done((f32[1,4,256,128]{3,2,1,0:T(8,128)S(1)}, f32[1,4,256,128]{3,2,1,0:T(8,128)}, u32[]{:S(2)}) %copy-start.2) | copy-done | bytes 524312
  3.9 0.0 copy-start.3
  3.9 1.0 %copy-done.3 = f32[1,4,256,128]{3,2,1,0:T(8,128)S(1)} copy-done((f32[1,4,256,128]{3,2,1,0:T(8,128)S(1)}, f32[1,4,256,128]{3,2,1,0:T(8,128)}, u32[]{:S(2)}) %copy-start.3) | copy-done | bytes 524312
  4.9 0.0 copy-start.4
  4.9 1.0 %copy-done.4 = f32[4,256,128]{2,1,0:T(8,128)S(1)} copy-done((f32[4,256,128]{2,1,0:T(8,128)S(1)}, f32[4,256,128]{2,1,0:T(8,128)}, u32[]{:S(2)}) %copy-start.4) | copy-done | bytes 524312
  5.9 26.4 %shard_map.91 = f32[2,128,64]{2,1,0:T(8,128)S(1)} custom-call(f32[1,2]{1,0:T(1,128)S(1)} %copy-done.5, s32[1,4]{1,0:T(1,128)S(1)} %copy-done.6, s32[1,3]{1,0:T(1,128)S(1)} %copy-done.7, s32[1]{0:T(128)S(6)} %copy.11.top_ref, f32[1,4,256,128]{3,2,1,0:T(8,128)S(1)} %copy-done, f32[1,4,256,128]{3,2,1,0:T(8,128)S(1)} %copy-done.1, ...), custom_call_target="tpu_custom_call" | custom-call | tf_op jit(solution)/shard_map/pallas_call | solution.py:262
  32.4 0.7 %copy.10 = f32[2,128,64]{1,2,0:T(8,128)} copy(f32[2,128,64]{2,1,0:T(8,128)S(1)} %shard_map.91) | data formatting | bytes 131072 | tf_op jit(solution)/shard_map/pallas_call | solution.py:262
Async XLA Ops:
  0.0 0.7 %copy-start.7 = (s32[1,3]{1,0:T(1,128)S(1)}, s32[1,3]{1,0:T(1,128)}, u32[]{:S(2)}) copy-start(s32[1,3]{1,0:T(1,128)} %src_ref.1) | copy-start | bytes 40
  0.0 0.7 %copy-start.6 = (s32[1,4]{1,0:T(1,128)S(1)}, s32[1,4]{1,0:T(1,128)}, u32[]{:S(2)}) copy-start(s32[1,4]{1,0:T(1,128)} %box_ref.1) | copy-start | bytes 52
  0.0 0.7 %copy-start.5 = (f32[1,2]{1,0:T(1,128)S(1)}, f32[1,2]{1,0:T(1,128)}, u32[]{:S(2)}) copy-start(f32[1,2]{1,0:T(1,128)} %wave_ref.1) | copy-start | bytes 28
  0.7 1.0 %copy-start = (f32[1,4,256,128]{3,2,1,0:T(8,128)S(1)}, f32[1,4,256,128]{3,2,1,0:T(8,128)}, u32[]{:S(2)}) copy-start(f32[1,4,256,128]{3,2,1,0:T(8,128)} %f0_hbm.1) | copy-start | bytes 1572868
  1.8 1.0 %copy-start.1 = (f32[1,4,256,128]{3,2,1,0:T(8,128)S(1)}, f32[1,4,256,128]{3,2,1,0:T(8,128)}, u32[]{:S(2)}) copy-start(f32[1,4,256,128]{3,2,1,0:T(8,128)} %f1_hbm.1) | copy-start | bytes 1572868
  2.8 1.0 %copy-start.2 = (f32[1,4,256,128]{3,2,1,0:T(8,128)S(1)}, f32[1,4,256,128]{3,2,1,0:T(8,128)}, u32[]{:S(2)}) copy-start(f32[1,4,256,128]{3,2,1,0:T(8,128)} %a3_hbm.1) | copy-start | bytes 1572868
  3.9 1.0 %copy-start.3 = (f32[1,4,256,128]{3,2,1,0:T(8,128)S(1)}, f32[1,4,256,128]{3,2,1,0:T(8,128)}, u32[]{:S(2)}) copy-start(f32[1,4,256,128]{3,2,1,0:T(8,128)} %a2_hbm.1) | copy-start | bytes 1572868
  4.9 1.0 %copy-start.4 = (f32[4,256,128]{2,1,0:T(8,128)S(1)}, f32[4,256,128]{2,1,0:T(8,128)}, u32[]{:S(2)}) copy-start(f32[4,256,128]{2,1,0:T(8,128)} %c_hbm.1) | copy-start | bytes 1572868

commit v2 on v1

v2 whole, which is shorter than its diff:
```python
import functools

import jax
import jax.numpy as jnp
from jax import lax
from jax.experimental import pallas as pl
from jax.experimental.pallas import tpu as pltpu
from jax.sharding import PartitionSpec as P

COEFFS = (-205.0 / 72.0, 8.0 / 5.0, -1.0 / 5.0, 8.0 / 315.0, -1.0 / 560.0)
MESH = pl.DeviceIdType.MESH
PAD = 8
LANES = 128
ROWS = 16


def kernel(
    shots, counts, wave_ref, box_ref, src_ref, top_ref, f0_hbm, f1_hbm, a3_hbm, a2_hbm, c_hbm, out_ref,
    now, mid, old, speed, image, strips_out, strips_in, own, fix, ring, band, coarse, arrived,
    load_sem, send_sem, recv_sem, shot_send, shot_recv,
):
    county, countx = counts
    nz, ny = speed.shape[0], speed.shape[1]
    half, quarter = ny // 2, ny // 4
    planes = [(f, z) for f in range(2) for z in range(nz)]
    gy, gx, shot = lax.axis_index("gy"), lax.axis_index("gx"), lax.axis_index("shot")
    has_up, has_down = gy > 0, gy < county - 1
    has_left, has_right = gx > 0, gx < countx - 1

    loads = [
        pltpu.make_async_copy(f1_hbm.at[0], now.at[0, :, pl.ds(PAD, ny), :], load_sem.at[0]),
        pltpu.make_async_copy(a2_hbm.at[0], now.at[1, :, pl.ds(PAD, ny), :], load_sem.at[1]),
        pltpu.make_async_copy(c_hbm, speed, load_sem.at[2]),
        pltpu.make_async_copy(f0_hbm.at[0], old.at[0], load_sem.at[3]),
        pltpu.make_async_copy(a3_hbm.at[0], old.at[1], load_sem.at[4]),
    ]
    for load in loads:
        load.start()

    barrier = pltpu.get_barrier_semaphore()
    sides = [
        (has_up, {"gy": gy - 1}),
        (has_down, {"gy": gy + 1}),
        (has_left, {"gx": gx - 1}),
        (has_right, {"gx": gx + 1}),
    ]
    for there, device in sides:
        @pl.when(there)
        def _(device=device):
            pl.semaphore_signal(barrier, inc=1, device_id=device, device_id_type=MESH)
    for step in range(1, shots):
        pl.semaphore_signal(
            barrier, inc=1, device_id={"shot": lax.rem(shot + step, shots)}, device_id_type=MESH
        )
    expected = shots - 1
    for there, _ in sides:
        expected = expected + there.astype(jnp.int32)

    nothing = jnp.zeros((2, nz, PAD, LANES), jnp.float32)
    for there, start in ((has_up, 0), (has_down, PAD + ny)):
        @pl.when(jnp.logical_not(there))
        def _(start=start):
            now[:, :, pl.ds(start, PAD), :] = nothing
            mid[:, :, pl.ds(start, PAD), :] = nothing
    for there, side in ((has_left, 0), (has_right, 1)):
        @pl.when(jnp.logical_not(there))
        def _(side=side):
            strips_in[:, side] = jnp.zeros((2, quarter, LANES), jnp.float32)

    lane = lax.broadcasted_iota(jnp.int32, (8, LANES), 1)
    group = lane // 8
    low = lax.rem(lane, 8) < 4
    edge = (lane < 4) | (lane >= LANES - 4)

    ri = lax.broadcasted_iota(jnp.int32, (LANES, LANES), 0)
    ci = lax.broadcasted_iota(jnp.int32, (LANES, LANES), 1)
    apart = jnp.abs(ri - ci)
    around = jnp.minimum(apart, LANES - apart)
    crossing = (ri // 8 == ci // 8) & ((lax.rem(ri, 8) < 4) != (lax.rem(ci, 8) < 4))
    weights = jnp.zeros((LANES, LANES), jnp.float32)
    crossed = weights
    for k in range(1, 5):
        weights = jnp.where(around == k, COEFFS[k], weights)
        crossed = jnp.where(crossing & (apart == k), COEFFS[k], crossed)
    for ref, whole in ((ring, weights), (band, crossed)):
        high = whole.astype(jnp.bfloat16)
        ref[0:LANES] = high
        ref[LANES : 2 * LANES] = high
        ref[2 * LANES : 3 * LANES] = (whole - high.astype(jnp.float32)).astype(jnp.bfloat16)

    def times(x, ref):
        high = x.astype(jnp.bfloat16)
        rest = (x - high.astype(jnp.float32)).astype(jnp.bfloat16)
        return jnp.dot(
            jnp.concatenate([high, rest, high], 1), ref[...], preferred_element_type=jnp.float32
        )

    def stencil(cells, at):
        centre = [cells[f, z, pl.ds(at + PAD, ROWS), :] for f, z in planes]
        along_x = times(jnp.concatenate(centre, 0), ring)
        result = []
        for p, (f, z) in enumerate(planes):
            total = along_x[p * ROWS : (p + 1) * ROWS] + (3.0 * COEFFS[0]) * centre[p]
            for k in range(1, 5):
                s = cells[f, z, pl.ds(at + (PAD + k), ROWS), :]
                s = s + cells[f, z, pl.ds(at + (PAD - k), ROWS), :]
                if z + k < nz:
                    s = s + centre[p + k]
                if z - k >= 0:
                    s = s + centre[p - k]
                total = total + COEFFS[k] * s
            result.append(total)
        return centre, result

    y0, y1, x0, x1 = box_ref[0, 0], box_ref[0, 1], box_ref[0, 2], box_ref[0, 3]
    sz, sy, sx = src_ref[0, 0], src_ref[0, 1], src_ref[0, 2]

    def place(at, rows):
        cell_y = gy * ny + at + lax.broadcasted_iota(jnp.int32, (rows, LANES), 0)
        cell_x = gx * LANES + lax.broadcasted_iota(jnp.int32, (rows, LANES), 1)
        inside = (cell_x >= x0) & (cell_x < x1) & (cell_y >= y0) & (cell_y < y1)
        return inside, (cell_x == sx) & (cell_y == sy)

    def amplitude(step, z):
        return jnp.where(sz == z, wave_ref[0, step], 0.0)

    def first_step(i, carry):
        at = pl.multiple_of(i * ROWS, ROWS)
        here = pl.ds(at, ROWS)
        inside, source = place(at, ROWS)
        centre, lap = stencil(now, at)
        for p, (f, z) in enumerate(planes):
            new = 2.0 * centre[p] - old[f, z, here, :] + speed[z, here, :] * lap[p]
            if f == 0:
                new = new + jnp.where(source, amplitude(0, z), 0.0)
            mid[f, z, pl.ds(at + PAD, ROWS), :] = jnp.where(inside, new, 0.0)
        return carry

    def second_step(i, carry):
        at = pl.multiple_of(i * ROWS, ROWS)
        here, padded = pl.ds(at, ROWS), pl.ds(at + PAD, ROWS)
        inside, source = place(at, ROWS)
        centre, lap = stencil(mid, at)
        total = None
        for z in range(nz):
            c = speed[z, here, :]
            f0, f1, a2 = old[0, z, here, :], now[0, z, padded, :], now[1, z, padded, :]
            f2, a1 = centre[z], centre[nz + z]
            f3 = 2.0 * f2 - f1 + c * lap[z] + jnp.where(source, amplitude(1, z), 0.0)
            f3 = jnp.where(inside, f3, 0.0)
            a0 = jnp.where(inside, 2.0 * a1 - a2 + c * lap[nz + z], 0.0)
            part = a0 * (f2 - 2.0 * f1 + f0) + a1 * (f3 - 2.0 * f2 + f1)
            total = part if z % 2 == 0 else total + part
            if z % 2 == 1:
                image[z // 2, here, :] = total
        return carry

    def spot(i, part, q):
        return pl.multiple_of(i * 8, 8) + (q * half + part * quarter)

    def packing(phase, value):
        def pack(i, carry):
            both = []
            for part in range(2):
                packed = jnp.zeros((8, LANES), jnp.float32)
                for q in range(2):
                    for p, cells in enumerate(value(i, part, q)):
                        base = q * 64 + p * 8
                        moved = pltpu.roll(cells, (base + 4) % LANES, 1)
                        packed = jnp.where(group == base // 8, moved, packed)
                own[pl.ds(pl.multiple_of(i * 8, 8) + part * quarter, 8), :] = packed
                both.append(packed)
            rows = pl.ds(pl.multiple_of(i * 8, 8), 8)
            strips_out[phase, 0, rows, :] = jnp.where(low, both[0], pltpu.roll(both[1], 4, 1))
            strips_out[phase, 1, rows, :] = jnp.where(
                low, pltpu.roll(both[0], LANES - 4, 1), both[1]
            )
            return carry

        lax.fori_loop(0, quarter // 8, pack, 0, unroll=2)

    def plain(i, part, q):
        return [now[f, z, pl.ds(spot(i, part, q) + PAD, 8), :] for f, z in planes]

    def fixes(i, part, q):
        packed = fix[pl.ds(pl.multiple_of(i * 8, 8) + part * quarter, 8), :]
        at = spot(i, part, q)
        inside, _ = place(at, 8)
        result = []
        for p, (f, z) in enumerate(planes):
            moved = pltpu.roll(packed, (124 - q * 64 - p * 8) % LANES, 1)
            result.append(jnp.where(inside & edge, speed[z, pl.ds(at, 8), :] * moved, 0.0))
        return result

    def fixed_middle(i, part, q):
        padded = pl.ds(spot(i, part, q) + PAD, 8)
        result = []
        for (f, z), lack in zip(planes, fixes(i, part, q)):
            value = mid[f, z, padded, :] + lack
            mid[f, z, padded, :] = value
            result.append(value)
        return result

    def fix_image(i, carry):
        for part in range(2):
            for q in range(2):
                at = spot(i, part, q)
                here, padded = pl.ds(at, 8), pl.ds(at + PAD, 8)
                lack = fixes(i, part, q)
                for z in range(0, nz, 2):
                    total = image[z // 2, here, :]
                    for d in (z, z + 1):
                        bent = mid[0, d, padded, :] - 2.0 * now[0, d, padded, :] + old[0, d, here, :]
                        total = total + lack[nz + d] * bent + mid[1, d, padded, :] * lack[d]
                    image[z // 2, here, :] = total
        return carry

    to = (has_down, has_up, has_right, has_left)
    came = (has_up, has_down, has_left, has_right)

    def exchange(cells, phase):
        def remote(index, src, dst, device):
            return pltpu.make_async_remote_copy(
                src_ref=src, dst_ref=dst,
                send_sem=send_sem.at[phase, index], recv_sem=recv_sem.at[phase, index],
                device_id=device, device_id_type=MESH,
            )

        first, last = pl.ds(PAD, PAD), pl.ds(ny, PAD)
        above, below = pl.ds(0, PAD), pl.ds(PAD + ny, PAD)
        return [
            remote(0, cells.at[:, :, last, :], cells.at[:, :, above, :], {"gy": gy + 1}),
            remote(1, cells.at[:, :, first, :], cells.at[:, :, below, :], {"gy": gy - 1}),
            remote(2, strips_out.at[phase, 0], strips_in.at[phase, 0], {"gx": gx + 1}),
            remote(3, strips_out.at[phase, 1], strips_in.at[phase, 1], {"gx": gx - 1}),
        ]

    def when(conditions, copies, action, which):
        for i in which:
            @pl.when(conditions[i])
            def _(i=i):
                getattr(copies[i], action)()

    def merge(phase):
        left, right = strips_in[phase, 0], strips_in[phase, 1]
        few = lax.rem(lax.broadcasted_iota(jnp.int32, (quarter, LANES), 1), 8) < 4
        both = jnp.concatenate(
            [
                jnp.where(few, left, pltpu.roll(right, 4, 1)),
                jnp.where(few, pltpu.roll(left, LANES - 4, 1), right),
            ],
            0,
        )
        fix[...] = times(both - own[...], band)

    chunks = ny // ROWS
    border = chunks - 1
    loads[0].wait()
    loads[1].wait()
    pl.semaphore_wait(barrier, expected)
    early = exchange(now, 0)
    when(to, early, "start", (0, 1))
    packing(0, plain)
    when(to, early, "start", (2, 3))
    for load in loads[2:]:
        load.wait()
    lax.fori_loop(1, border, first_step, 0)
    when(came, early, "wait_recv", (0, 1))
    lax.fori_loop(0, 2, lambda i, carry: first_step(i * border, carry), 0)
    when(came, early, "wait_recv", (2, 3))
    merge(0)
    packing(1, fixed_middle)

    late = exchange(mid, 1)
    when(to, late, "start", (2, 3, 0, 1))
    lax.fori_loop(1, border, second_step, 0)
    when(came, late, "wait_recv", (0, 1))
    lax.fori_loop(0, 2, lambda i, carry: second_step(i * border, carry), 0)
    when(came, late, "wait_recv", (2, 3))
    merge(1)
    lax.fori_loop(0, quarter // 8, fix_image, 0)

    pair = lax.broadcasted_iota(jnp.int32, (LANES, LANES), 0) // 2
    column = lax.broadcasted_iota(jnp.int32, (LANES, LANES), 1)
    total = None
    for k in range(nz // 2):
        rows = image[k, pl.ds(0, half, stride=2), :] + image[k, pl.ds(1, half, stride=2), :]
        pick = (column == pair + 64 * k).astype(jnp.float32)
        part = jnp.dot(rows, pick, precision=lax.Precision.HIGHEST, preferred_element_type=jnp.float32)
        total = part if total is None else total + part
    coarse[...] = total
    sends = []
    for step in range(1, shots):
        copy = pltpu.make_async_remote_copy(
            src_ref=coarse, dst_ref=arrived.at[step - 1],
            send_sem=shot_send.at[step - 1], recv_sem=shot_recv.at[step - 1],
            device_id={"shot": lax.rem(shot + step, shots)}, device_id_type=MESH,
        )
        copy.start()
        sends.append(copy)
    for step, copy in enumerate(sends):
        copy.wait_recv()
        total = total + arrived[step]
    depth = top_ref[0].astype(jnp.float32)
    for k in range(nz // 2):
        factor = (0.25 + (depth + (2.0 * k + 1.0)) / 128.0) * 0.125
        out_ref[k] = total[:, 64 * k : 64 * k + 64] * factor
    for copy in sends:
        copy.wait_send()
    when(to, early, "wait_send", range(4))
    when(to, late, "wait_send", range(4))


def per_device(shots, counts, fwd_prev, fwd_cur, adj_late, adj_now, courant, wavelet, boxes, sources, slab_top):
    nz, ny, nx = courant.shape
    f32 = jnp.float32
    smem = pl.BlockSpec(memory_space=pltpu.SMEM)
    hbm = pl.BlockSpec(memory_space=pltpu.HBM)
    return pl.pallas_call(
        functools.partial(kernel, shots, counts),
        out_shape=jax.ShapeDtypeStruct((nz // 2, ny // 2, nx // 2), f32),
        in_specs=[smem] * 4 + [hbm] * 5,
        out_specs=pl.BlockSpec(memory_space=pltpu.VMEM),
        scratch_shapes=[
            pltpu.VMEM((2, nz, ny + 2 * PAD, nx), f32),
            pltpu.VMEM((2, nz, ny + 2 * PAD, nx), f32),
            pltpu.VMEM((2, nz, ny, nx), f32),
            pltpu.VMEM((nz, ny, nx), f32),
            pltpu.VMEM((nz // 2, ny, nx), f32),
            pltpu.VMEM((2, 2, ny // 4, nx), f32),
            pltpu.VMEM((2, 2, ny // 4, nx), f32),
            pltpu.VMEM((ny // 2, nx), f32),
            pltpu.VMEM((ny // 2, nx), f32),
            pltpu.VMEM((3 * nx, nx), jnp.bfloat16),
            pltpu.VMEM((3 * nx, nx), jnp.bfloat16),
            pltpu.VMEM((ny // 2, nx), f32),
            pltpu.VMEM((max(shots - 1, 1), ny // 2, nx), f32),
            pltpu.SemaphoreType.DMA((5,)),
            pltpu.SemaphoreType.DMA((2, 4)),
            pltpu.SemaphoreType.DMA((2, 4)),
            pltpu.SemaphoreType.DMA((max(shots - 1, 1),)),
            pltpu.SemaphoreType.DMA((max(shots - 1, 1),)),
        ],
        compiler_params=pltpu.CompilerParams(
            collective_id=0, has_side_effects=True, vmem_limit_bytes=56 * 1024 * 1024
        ),
    )(wavelet, boxes, sources, slab_top, fwd_prev, fwd_cur, adj_late, adj_now, courant)


def solution(mesh):
    shots = mesh.shape["shot"]
    counts = (mesh.shape["gy"], mesh.shape["gx"])
    return jax.shard_map(
        functools.partial(per_device, shots, counts),
        mesh=mesh,
        in_specs=(
            P("shot", None, "gy", "gx"),
            P("shot", None, "gy", "gx"),
            P("shot", None, "gy", "gx"),
            P("shot", None, "gy", "gx"),
            P(None, "gy", "gx"),
            P("shot", None),
            P("shot", None),
            P("shot", None),
            P(),
        ),
        out_specs=P(None, "gy", "gx"),
        check_vma=False,
    )
```

time: 33.4 us -> 19.1 us (0.57)
  Pallas kernels: 26.4 us -> 16.7 us
  local copies, waits for them, and re-layouts: 5.92 us -> 1.62 us
    pallas_call x1, Pallas kernels: 26.4 us -> 16.7 us  [per_device(): pl.pallas_call(functools.partial(kernel, shots, counts), out_shape=jax.Sh...]
    unnamed x16 -> x0, local copies, waits for them, and re-layouts: 5.21 us -> none
    pallas_call x1, local copies, waits for them, and re-layouts: 0.71 us -> 1.62 us  [per_device(): pl.pallas_call(functools.partial(kernel, shots, counts), out_shape=jax.Sh...]
where the time goes in v2:
time: 19.1 us; the launch traced here: 19 us
  Pallas kernels  16.7 us (87%)
  local copies, waits for them, and re-layouts  1.62 us (8%)
  between operations  0.66 us (3%)
    pallas_call x1, Pallas kernels, per_device(): pl.pallas_call(functools.partial(kernel, shots, counts), out_shape=jax.Sh...  16.7 us
    pallas_call x1, local copies, waits for them, and re-layouts, per_device(): pl.pallas_call(functools.partial(kernel, shots, counts), out_shape=jax.Sh...  1.62 us

profile of v2, /device:TPU:0, one launch (start us, length us, event | category | flops | bytes accessed | tf_op | source)
XLA Modules:
  0.0 19.0 jit_solution(16276657945123050929)
XLA Ops:
  0.7 16.7 %shard_map.91 = f32[2,128,64]{2,1,0:T(8,128)} custom-call(f32[1,2]{1,0:T(1,128)} %wave_ref.1, s32[1,4]{1,0:T(1,128)} %box_ref.1, s32[1,3]{1,0:T(1,128)} %src_ref.1, s32[1]{0:T(128)S(6)} %copy.11.top_ref, f32[1,4,256,128]{3,2,1,0:T(8,128)} %f0_hbm.1, f32[1,4,256,128]{3,2,1,0:T(8,128)} %f1_hbm.1, f32[1,4,256,128]{3,2,1,0:T(8,128)} %a3_hbm.1, ...), custom_call_target="tpu_custom_call" | custom-call | tf_op jit(solution)/shard_map/pallas_call | solution.py:319
  17.3 1.6 %copy.10 = f32[2,128,64]{1,2,0:T(8,128)} copy(f32[2,128,64]{2,1,0:T(8,128)} %shard_map.91) | data formatting | bytes 131072 | tf_op jit(solution)/shard_map/pallas_call | solution.py:319

commit v3 on v2

--- a/solution.py
+++ b/solution.py
@@ -286,7 +286,10 @@
     for k in range(nz // 2):
         rows = image[k, pl.ds(0, half, stride=2), :] + image[k, pl.ds(1, half, stride=2), :]
         pick = (column == pair + 64 * k).astype(jnp.float32)
-        part = jnp.dot(rows, pick, precision=lax.Precision.HIGHEST, preferred_element_type=jnp.float32)
+        part = lax.dot_general(
+            pick, rows, (((0,), (1,)), ((), ())),
+            precision=lax.Precision.HIGHEST, preferred_element_type=jnp.float32,
+        )
         total = part if total is None else total + part
     coarse[...] = total
     sends = []
@@ -304,7 +307,7 @@
     depth = top_ref[0].astype(jnp.float32)
     for k in range(nz // 2):
         factor = (0.25 + (depth + (2.0 * k + 1.0)) / 128.0) * 0.125
-        out_ref[k] = total[:, 64 * k : 64 * k + 64] * factor
+        out_ref[k] = total[64 * k : 64 * k + 64] * factor
     for copy in sends:
         copy.wait_send()
     when(to, early, "wait_send", range(4))
@@ -316,9 +319,9 @@
     f32 = jnp.float32
     smem = pl.BlockSpec(memory_space=pltpu.SMEM)
     hbm = pl.BlockSpec(memory_space=pltpu.HBM)
-    return pl.pallas_call(
+    out = pl.pallas_call(
         functools.partial(kernel, shots, counts),
-        out_shape=jax.ShapeDtypeStruct((nz // 2, ny // 2, nx // 2), f32),
+        out_shape=jax.ShapeDtypeStruct((nz // 2, nx // 2, ny // 2), f32),
         in_specs=[smem] * 4 + [hbm] * 5,
         out_specs=pl.BlockSpec(memory_space=pltpu.VMEM),
         scratch_shapes=[
@@ -333,8 +336,8 @@
             pltpu.VMEM((ny // 2, nx), f32),
             pltpu.VMEM((3 * nx, nx), jnp.bfloat16),
             pltpu.VMEM((3 * nx, nx), jnp.bfloat16),
-            pltpu.VMEM((ny // 2, nx), f32),
-            pltpu.VMEM((max(shots - 1, 1), ny // 2, nx), f32),
+            pltpu.VMEM((nx, ny // 2), f32),
+            pltpu.VMEM((max(shots - 1, 1), nx, ny // 2), f32),
             pltpu.SemaphoreType.DMA((5,)),
             pltpu.SemaphoreType.DMA((2, 4)),
             pltpu.SemaphoreType.DMA((2, 4)),
@@ -342,9 +345,10 @@
             pltpu.SemaphoreType.DMA((max(shots - 1, 1),)),
         ],
         compiler_params=pltpu.CompilerParams(
-            collective_id=0, has_side_effects=True, vmem_limit_bytes=56 * 1024 * 1024
+            collective_id=0, has_side_effects=True, vmem_limit_bytes=54912 * 1024
         ),
     )(wavelet, boxes, sources, slab_top, fwd_prev, fwd_cur, adj_late, adj_now, courant)
+    return jnp.swapaxes(out, 1, 2)
 
 
 def solution(mesh):

time: 19.1 us -> 17.6 us (0.921)
  local copies, waits for them, and re-layouts: 1.62 us -> 0.64 us
  Pallas kernels: 16.7 us -> 16 us
    pallas_call x1 -> x0, local copies, waits for them, and re-layouts: 1.62 us -> none  [per_device(): pl.pallas_call(functools.partial(kernel, shots, counts), out_shape=jax.Sh...]
    unnamed x0 -> x7, local copies, waits for them, and re-layouts: none -> 0.64 us
    pallas_call x1, Pallas kernels: 16.7 us -> 16 us  [per_device(): pl.pallas_call(functools.partial(kernel, shots, counts), out_shape=jax.Sh...]
where the time goes in v3:
time: 17.6 us; the launch traced here: 17.4 us
  Pallas kernels  16 us (91%)
  between operations  0.73 us (4%)
  local copies, waits for them, and re-layouts  0.64 us (4%)
    pallas_call x1, Pallas kernels, per_device(): pl.pallas_call(functools.partial(kernel, shots, counts), out_shape=jax.Sh...  16 us
    unnamed x7, local copies, waits for them, and re-layouts  0.64 us

profile of v3, /device:TPU:0, one launch (start us, length us, event | category | flops | bytes accessed | tf_op | source)
XLA Modules:
  0.0 17.4 jit_solution(16676974497284588157)
XLA Ops:
  0.0 0.0 copy-start.2
  0.0 0.0 copy-start.1
  0.0 0.0 copy-start
  0.7 0.0 copy-done.2
  0.7 0.0 copy-done.1
  0.7 0.0 copy-done
  0.7 16.0 %shard_map.91 = f32[2,64,128]{2,1,0:T(8,128)S(1)} custom-call(f32[1,2]{1,0:T(1,128)S(1)} %copy-done, s32[1,4]{1,0:T(1,128)S(1)} %copy-done.1, s32[1,3]{1,0:T(1,128)S(1)} %copy-done.2, s32[1]{0:T(128)S(6)} %copy.11.top_ref, f32[1,4,256,128]{3,2,1,0:T(8,128)} %f0_hbm.1, f32[1,4,256,128]{3,2,1,0:T(8,128)} %f1_hbm.1, f32[1,4,256,128]{3,2,1,0:T(8,128)} %a3_hbm.1, ...), custom_call_target="tpu_custom_call" | custom-call | tf_op jit(solution)/shard_map/pallas_call | solution.py:322
  16.8 0.6 %copy.12 = f32[2,128,64]{1,2,0:T(8,128)} copy(f32[2,128,64]{1,2,0:T(8,128)S(1)} %bitcast.1) | data formatting | bytes 131072
Async XLA Ops:
  0.0 0.7 %copy-start.2 = (s32[1,3]{1,0:T(1,128)S(1)}, s32[1,3]{1,0:T(1,128)}, u32[]{:S(2)}) copy-start(s32[1,3]{1,0:T(1,128)} %src_ref.1) | copy-start | bytes 40
  0.0 0.7 %copy-start.1 = (s32[1,4]{1,0:T(1,128)S(1)}, s32[1,4]{1,0:T(1,128)}, u32[]{:S(2)}) copy-start(s32[1,4]{1,0:T(1,128)} %box_ref.1) | copy-start | bytes 52
  0.0 0.7 %copy-start = (f32[1,2]{1,0:T(1,128)S(1)}, f32[1,2]{1,0:T(1,128)}, u32[]{:S(2)}) copy-start(f32[1,2]{1,0:T(1,128)} %wave_ref.1) | copy-start | bytes 28

commit v4 on v3

--- a/solution.py
+++ b/solution.py
@@ -265,20 +265,20 @@
     for load in loads[2:]:
         load.wait()
     lax.fori_loop(1, border, first_step, 0)
-    when(came, early, "wait_recv", (0, 1))
-    lax.fori_loop(0, 2, lambda i, carry: first_step(i * border, carry), 0)
-    when(came, early, "wait_recv", (2, 3))
+    when(came, early, "wait_recv", range(4))
     merge(0)
+    first_step(0, 0)
+    first_step(border, 0)
     packing(1, fixed_middle)
 
     late = exchange(mid, 1)
     when(to, late, "start", (2, 3, 0, 1))
     lax.fori_loop(1, border, second_step, 0)
-    when(came, late, "wait_recv", (0, 1))
-    lax.fori_loop(0, 2, lambda i, carry: second_step(i * border, carry), 0)
-    when(came, late, "wait_recv", (2, 3))
+    when(came, late, "wait_recv", range(4))
     merge(1)
-    lax.fori_loop(0, quarter // 8, fix_image, 0)
+    second_step(0, 0)
+    second_step(border, 0)
+    lax.fori_loop(0, quarter // 8, fix_image, 0, unroll=4)
 
     pair = lax.broadcasted_iota(jnp.int32, (LANES, LANES), 0) // 2
     column = lax.broadcasted_iota(jnp.int32, (LANES, LANES), 1)

time: 17.6 us -> 17 us (0.966)
  Pallas kernels: 16 us -> 15.4 us
    pallas_call x1, Pallas kernels: 16 us -> 15.4 us  [per_device(): pl.pallas_call(functools.partial(kernel, shots, counts), out_shape=jax.Sh...]
where the time goes in v4:
time: 17 us; the launch traced here: 16.8 us
  Pallas kernels  15.4 us (91%)
  between operations  0.73 us (4%)
  local copies, waits for them, and re-layouts  0.64 us (4%)
    pallas_call x1, Pallas kernels, per_device(): pl.pallas_call(functools.partial(kernel, shots, counts), out_shape=jax.Sh...  15.4 us
    unnamed x7, local copies, waits for them, and re-layouts  0.64 us

profile of v4, /device:TPU:0, one launch (start us, length us, event | category | flops | bytes accessed | tf_op | source)
XLA Modules:
  0.0 16.8 jit_solution(6645455387908423599)
XLA Ops:
  0.0 0.0 copy-start.2
  0.0 0.0 copy-start.1
  0.0 0.0 copy-start
  0.7 0.0 copy-done.2
  0.7 0.0 copy-done.1
  0.7 0.0 copy-done
  0.7 15.4 %shard_map.91 = f32[2,64,128]{2,1,0:T(8,128)S(1)} custom-call(f32[1,2]{1,0:T(1,128)S(1)} %copy-done, s32[1,4]{1,0:T(1,128)S(1)} %copy-done.1, s32[1,3]{1,0:T(1,128)S(1)} %copy-done.2, s32[1]{0:T(128)S(6)} %copy.11.top_ref, f32[1,4,256,128]{3,2,1,0:T(8,128)} %f0_hbm.1, f32[1,4,256,128]{3,2,1,0:T(8,128)} %f1_hbm.1, f32[1,4,256,128]{3,2,1,0:T(8,128)} %a3_hbm.1, ...), custom_call_target="tpu_custom_call" | custom-call | tf_op jit(solution)/shard_map/pallas_call | solution.py:322
  16.2 0.6 %copy.12 = f32[2,128,64]{1,2,0:T(8,128)} copy(f32[2,128,64]{1,2,0:T(8,128)S(1)} %bitcast.1) | data formatting | bytes 131072
Async XLA Ops:
  0.0 0.7 %copy-start.2 = (s32[1,3]{1,0:T(1,128)S(1)}, s32[1,3]{1,0:T(1,128)}, u32[]{:S(2)}) copy-start(s32[1,3]{1,0:T(1,128)} %src_ref.1) | copy-start | bytes 40
  0.0 0.7 %copy-start.1 = (s32[1,4]{1,0:T(1,128)S(1)}, s32[1,4]{1,0:T(1,128)}, u32[]{:S(2)}) copy-start(s32[1,4]{1,0:T(1,128)} %box_ref.1) | copy-start | bytes 52
  0.0 0.7 %copy-start = (f32[1,2]{1,0:T(1,128)S(1)}, f32[1,2]{1,0:T(1,128)}, u32[]{:S(2)}) copy-start(f32[1,2]{1,0:T(1,128)} %wave_ref.1) | copy-start | bytes 28

commit v5 on v4

--- a/solution.py
+++ b/solution.py
@@ -285,11 +285,15 @@
     total = None
     for k in range(nz // 2):
         rows = image[k, pl.ds(0, half, stride=2), :] + image[k, pl.ds(1, half, stride=2), :]
-        pick = (column == pair + 64 * k).astype(jnp.float32)
-        part = lax.dot_general(
-            pick, rows, (((0,), (1,)), ((), ())),
-            precision=lax.Precision.HIGHEST, preferred_element_type=jnp.float32,
-        )
+        pick = (column == pair + 64 * k).astype(jnp.bfloat16)
+        left, part = rows, None
+        for _ in range(3):
+            piece = left.astype(jnp.bfloat16)
+            left = left - piece.astype(jnp.float32)
+            term = lax.dot_general(
+                pick, piece, (((0,), (1,)), ((), ())), preferred_element_type=jnp.float32
+            )
+            part = term if part is None else part + term
         total = part if total is None else total + part
     coarse[...] = total
     sends = []

time: 17 us -> 16.8 us (0.988)
  no operation moved by 1% of the time
where the time goes in v5:
time: 16.8 us; the launch traced here: 16.7 us
  Pallas kernels  15.3 us (91%)
  between operations  0.73 us (4%)
  local copies, waits for them, and re-layouts  0.64 us (4%)
    pallas_call x1, Pallas kernels, per_device(): pl.pallas_call(functools.partial(kernel, shots, counts), out_shape=jax.Sh...  15.3 us
    unnamed x7, local copies, waits for them, and re-layouts  0.64 us

profile of v5, /device:TPU:0, one launch (start us, length us, event | category | flops | bytes accessed | tf_op | source)
XLA Modules:
  0.0 16.7 jit_solution(5525515257241928050)
XLA Ops:
  0.0 0.0 copy-start.2
  0.0 0.0 copy-start.1
  0.0 0.0 copy-start
  0.7 0.0 copy-done.2
  0.7 0.0 copy-done.1
  0.7 0.0 copy-done
  0.7 15.3 %shard_map.91 = f32[2,64,128]{2,1,0:T(8,128)S(1)} custom-call(f32[1,2]{1,0:T(1,128)S(1)} %copy-done, s32[1,4]{1,0:T(1,128)S(1)} %copy-done.1, s32[1,3]{1,0:T(1,128)S(1)} %copy-done.2, s32[1]{0:T(128)S(6)} %copy.11.top_ref, f32[1,4,256,128]{3,2,1,0:T(8,128)} %f0_hbm.1, f32[1,4,256,128]{3,2,1,0:T(8,128)} %f1_hbm.1, f32[1,4,256,128]{3,2,1,0:T(8,128)} %a3_hbm.1, ...), custom_call_target="tpu_custom_call" | custom-call | tf_op jit(solution)/shard_map/pallas_call | solution.py:326
  16.0 0.6 %copy.12 = f32[2,128,64]{1,2,0:T(8,128)} copy(f32[2,128,64]{1,2,0:T(8,128)S(1)} %bitcast.1) | data formatting | bytes 131072
Async XLA Ops:
  0.0 0.7 %copy-start.2 = (s32[1,3]{1,0:T(1,128)S(1)}, s32[1,3]{1,0:T(1,128)}, u32[]{:S(2)}) copy-start(s32[1,3]{1,0:T(1,128)} %src_ref.1) | copy-start | bytes 40
  0.0 0.7 %copy-start.1 = (s32[1,4]{1,0:T(1,128)S(1)}, s32[1,4]{1,0:T(1,128)}, u32[]{:S(2)}) copy-start(s32[1,4]{1,0:T(1,128)} %box_ref.1) | copy-start | bytes 52
  0.0 0.7 %copy-start = (f32[1,2]{1,0:T(1,128)S(1)}, f32[1,2]{1,0:T(1,128)}, u32[]{:S(2)}) copy-start(f32[1,2]{1,0:T(1,128)} %wave_ref.1) | copy-start | bytes 28
